TPU v7x, 32 devices: a whole 2x2x4 slice. The times are simulated.
32 devices in a mesh: groups: 2 (over y), pert: 4 (over z), lat: 2 (over x), fld: 2 (over core).
Axes of the slice: x: 2, y: 2, z: 4, core: 2. Of those that a mesh axis runs over, the one named last changes fastest.
Arguments:
- perturb: float32 [64, 4, 32, 1024], P(('groups', 'pert', 'fld'), None, 'lat'), parts along dimension 0, may hold values from -6 to 6
- traj_store: float32 [8, 4, 32, 1024], P(('groups', 'pert'), 'fld', 'lat'), parts along dimension 0
- owners: int32 [6], P('groups'), parts along dimension 0, may hold values from 0 to 3, as said below
Outputs:
- advanced: float32 [64, 4, 32, 1024], P(('groups', 'pert', 'fld'), None, 'lat'), parts along dimension 0
There are 2 independent parts, one for each index of `groups`. A program takes and returns all parts, laid end to end along the dimension named above; each array names one. Nothing has to cross between parts.
Inputs may be any that keep to these rules, and one draw needn't show every extreme that they name: `owners`: the 3 slots are distinct.
All inputs are finite; a program needn't handle non-finite values.
Results may differ from a plain program's by a relative error of at most 0.00002.
Values sent between devices are 32-bit elements; how exact they have to be, the bound alone decides.
A program may use at most 64 MiB of HBM per device.

v0:
```python
import jax
import jax.numpy as jnp
from jax import lax
from jax.sharding import PartitionSpec as P

STEPS = 6


time_step = 0.1
gravity = 1.0


def broadcast(value, axis, source):
    kept = jnp.where(lax.axis_index(axis) == source, value, 0).astype(value.dtype)
    return lax.psum(kept, axis)


def padded_2(value, sides, width):
    for axis, dim in sides:
        devices, length = (lax.axis_size(axis), value.shape[dim])
        up = [(i, (i + 1) % devices) for i in range(devices - 1)]
        down = [(j, i) for i, j in up]
        last = lax.slice_in_dim(value, length - width, length, axis=dim)
        first = lax.slice_in_dim(value, 0, width, axis=dim)
        before = lax.ppermute(last, axis, up)
        after = lax.ppermute(first, axis, down)
        value = jnp.concatenate([before, value, after], axis=dim)
    return value


def advance(padded, coef, coriolis):
    centre = padded[..., 1:-1, :]
    north = padded[..., 2:, :]
    south = padded[..., :-2, :]
    east = jnp.roll(centre, -1, axis=-1)
    west = jnp.roll(centre, 1, axis=-1)
    grad_x = (east - west) * 0.5
    grad_y = (north - south) * 0.5
    spread = east + west + north + south - 4.0 * centre
    tend = -(coef[0] * grad_x + coef[1] * grad_y) + coef[3] * spread
    diverge = grad_x[..., 1, :, :] + grad_y[..., 2, :, :]
    height = tend[..., 0, :, :] - coef[2] * diverge
    zonal = tend[..., 1, :, :] - gravity * grad_x[..., 0, :, :] + coriolis * centre[..., 2, :, :]
    merid = tend[..., 2, :, :] - gravity * grad_y[..., 0, :, :] - coriolis * centre[..., 1, :, :]
    tracer = tend[..., 3, :, :] - 0.5 * diverge
    return centre + time_step * jnp.stack([height, zonal, merid, tracer], axis=-3)


def interpolate(records, which):
    earlier = which // 3
    weight = which % 3 / 3.0
    return (1.0 - weight) * records[earlier] + weight * records[earlier + 1]


def coriolis_rows(global_rows, total_rows):
    return jnp.sin(jnp.pi * ((global_rows.astype(jnp.float32) + 0.5) / total_rows - 0.5))[:, None]


def per_device(perturb, traj_store, owners):
    rows = perturb.shape[2]
    total_rows = rows * lax.axis_size("lat")
    first_row = lax.axis_index("lat") * rows
    halves = []
    for record in range(owners.shape[0]):
        halves.append(broadcast(traj_store[0], "pert", owners[record]))
    records = lax.all_gather(jnp.stack(halves), "fld", axis=1, tiled=True)
    state = perturb
    coriolis = coriolis_rows(first_row + jnp.arange(rows, dtype=jnp.int32), total_rows)
    for which in range(STEPS):
        padded = padded_2(state, (("lat", 2),), 1)
        state = advance(padded, interpolate(records, which), coriolis)
    return state


def solution(mesh):
    in_specs = (
        P(("groups", "pert", "fld"), None, "lat", None),
        P(("groups", "pert"), "fld", "lat", None),
        P("groups"),
    )
    out_specs = P(("groups", "pert", "fld"), None, "lat", None)
    return jax.shard_map(
        per_device, mesh=mesh, in_specs=in_specs, out_specs=out_specs, check_vma=False
    )
```

profile of v0, /device:TPU:0, one launch (start us, length us, event | category | flops | bytes accessed | tf_op | source)
XLA Modules:
  0.0 126.1 jit_solution(9172664070301005086)
XLA Ops:
  6.5 2.0 %fusion.71 = (f32[4,4,1,1024]{3,2,1,0:T(1,128)}, f32[4,4,1,1024]{3,2,1,0:T(1,128)}) fusion(f32[4,4,16,1024]{3,2,1,0:T(8,128)} %param.3), kind=kLoop, calls=%fused_computation.182 | loop fusion | bytes 262144 | tf_op jit(solution)/shard_map/slice | solution.py:23
  8.6 4.8 %collective-permute-start.1 = (f32[4,4,1,1024]{3,2,1,0:T(1,128)}, f32[4,4,1,1024]{3,2,1,0:T(1,128)S(1)}, u32[]{:S(2)}, u32[]{:S(2)}) collective-permute-start(f32[4,4,1,1024]{3,2,1,0:T(1,128)} %get-tuple-element.90), channel_id=1, source_target_pairs={{0,2},{1,3},{4,6},{5,7},{8,10},{9,11},{12,14},{13,15},{16,18},{17,... | collective-permute-start | bytes 196616 | tf_op jit(solution)/shard_map/ppermute | solution.py:25
  13.4 1.3 %collective-permute-start = (f32[4,4,1,1024]{3,2,1,0:T(1,128)}, f32[4,4,1,1024]{3,2,1,0:T(1,128)S(1)}, u32[]{:S(2)}, u32[]{:S(2)}) collective-permute-start(f32[4,4,1,1024]{3,2,1,0:T(1,128)} %get-tuple-element.91), channel_id=1, source_target_pairs={{2,0},{3,1},{6,4},{7,5},{10,8},{11,9},{14,12},{15,13},{18,16},{19,... | collective-permute-start | bytes 196616 | tf_op jit(solution)/shard_map/ppermute | solution.py:26
  14.7 1.4 %fusion.72 = (s32[1]{0:T(128)}, s32[1]{0:T(128)}, s32[1]{0:T(128)}) fusion(s32[3]{0:T(128)} %param.5), kind=kLoop, calls=%fused_computation.183 | loop fusion | bytes 24 | tf_op jit(solution)/shard_map/slice | solution.py:65
  18.0 1.7 %broadcast_select_fusion.2 = (f32[1,2,16,1024]{3,2,1,0:T(8,128)}, f32[1,2,16,1024]{3,2,1,0:T(8,128)}, f32[1,2,16,1024]{3,2,1,0:T(8,128)}) fusion(f32[1,2,16,1024]{3,2,1,0:T(8,128)} %param.4, pred[]{:T(512)S(6)} %eq.9, pred[]{:T(512)S(6)} %eq.11, pred[]{:T(512)S(6)} %eq.10), kind=kLoop, calls=%fused_computation.163 | loop fusion | flops 98304 | bytes 524291 | tf_op jit(solution)/shard_map/jit(_where)/select_n | solution.py:14
  19.7 0.4 fusion.69
  20.3 1.3 %fusion.7 = f32[4,4,16,1024]{3,2,1,0:T(8,128)} fusion(f32[4,4,1,1024]{3,2,1,0:T(1,128)S(1)} %collective-permute-done, f32[4,4,16,1024]{3,2,1,0:T(8,128)S(1)} %copy-done, f32[4,4,1,1024]{3,2,1,0:T(1,128)S(1)} %collective-permute-done.1), kind=kLoop, calls=%fused_computation.43 | loop fusion | flops 1048576 | bytes 2228224 | tf_op jit(solution)/shard_map/mul | solution.py:38
  21.6 38.0 %all-reduce.3.cloned.1.call-done = (f32[1,2,16,1024]{3,2,1,0:T(8,128)}, f32[1,2,16,1024]{3,2,1,0:T(8,128)}, f32[1,2,16,1024]{3,2,1,0:T(8,128)}) async-done(((f32[1,2,16,1024]{3,2,1,0:T(8,128)}, f32[1,2,16,1024]{3,2,1,0:T(8,128)}, f32[1,2,16,1024]{3,2,1,0:T(8,128)}), (f32[1,2,16,1024]{3,2,1,0:T(8,128)}, f32[1,2,16,1024]{3,2,1,0:T(8,128)}, f32[1,2,16,1024]{3,2,1,0:T(8,128)})) %all-reduce.3.cloned.1.call-update) | async-done | bytes 393232 | tf_op jit(solution)/shard_map/psum | solution.py:15
  59.6 1.1 pad_maximum_fusion.24
  60.6 2.4 %all_gather.3 = f32[3,4,16,1024]{3,2,1,0:T(8,128)S(1)} all-gather(f32[3,2,16,1024]{3,2,1,0:T(8,128)S(1)} %pad_maximum_fusion.24), channel_id=1, replica_groups=mesh['groups'=2,'pert'=4,'lat'=2,'fld'=2] {'fld'}, dimensions={1}, use_global_device_ids=true | all-gather | bytes 1179648 | tf_op jit(solution)/shard_map/all_gather | solution.py:66
  63.3 0.8 fusion.29
  64.1 0.4 copy-done.1
  65.0 0.4 fusion.66
  65.6 3.3 %collective-permute-start.3 = (f32[4,4,1,1024]{3,2,1,0:T(1,128)S(1)}, f32[4,4,1,1024]{3,2,1,0:T(1,128)S(1)}, u32[]{:S(2)}, u32[]{:S(2)}) collective-permute-start(f32[4,4,1,1024]{3,2,1,0:T(1,128)S(1)} %get-tuple-element.84), channel_id=1, source_target_pairs={{0,2},{1,3},{4,6},{5,7},{8,10},{9,11},{12,14},{13,15},{16,18},{17,... | collective-permute-start | bytes 196616 | tf_op jit(solution)/shard_map/ppermute | solution.py:25
  68.9 1.3 %collective-permute-start.2 = (f32[4,4,1,1024]{3,2,1,0:T(1,128)S(1)}, f32[4,4,1,1024]{3,2,1,0:T(1,128)S(1)}, u32[]{:S(2)}, u32[]{:S(2)}) collective-permute-start(f32[4,4,1,1024]{3,2,1,0:T(1,128)S(1)} %get-tuple-element.85), channel_id=1, source_target_pairs={{2,0},{3,1},{6,4},{7,5},{10,8},{11,9},{14,12},{15,13},{18,16},{19,... | collective-permute-start | bytes 196616 | tf_op jit(solution)/shard_map/ppermute | solution.py:26
  70.4 0.5 collective-permute-done.3
  70.8 4.3 %collective-permute-done.2 = f32[4,4,1,1024]{3,2,1,0:T(1,128)S(1)} collective-permute-done((f32[4,4,1,1024]{3,2,1,0:T(1,128)S(1)}, f32[4,4,1,1024]{3,2,1,0:T(1,128)S(1)}, u32[]{:S(2)}, u32[]{:S(2)}) %collective-permute-start.2) | collective-permute-done | bytes 65568 | tf_op jit(solution)/shard_map/ppermute | solution.py:26
  75.4 0.8 fusion.27
  76.3 0.3 fusion.39
  76.6 0.3 fusion.1
  76.9 0.4 fusion.63
  77.4 1.6 %collective-permute-start.5 = (f32[4,4,1,1024]{3,2,1,0:T(1,128)S(1)}, f32[4,4,1,1024]{3,2,1,0:T(1,128)S(1)}, u32[]{:S(2)}, u32[]{:S(2)}) collective-permute-start(f32[4,4,1,1024]{3,2,1,0:T(1,128)S(1)} %get-tuple-element.78), channel_id=1, source_target_pairs={{0,2},{1,3},{4,6},{5,7},{8,10},{9,11},{12,14},{13,15},{16,18},{17,... | collective-permute-start | bytes 196616 | tf_op jit(solution)/shard_map/ppermute | solution.py:25
  79.0 1.3 %collective-permute-start.4 = (f32[4,4,1,1024]{3,2,1,0:T(1,128)S(1)}, f32[4,4,1,1024]{3,2,1,0:T(1,128)S(1)}, u32[]{:S(2)}, u32[]{:S(2)}) collective-permute-start(f32[4,4,1,1024]{3,2,1,0:T(1,128)S(1)} %get-tuple-element.79), channel_id=1, source_target_pairs={{2,0},{3,1},{6,4},{7,5},{10,8},{11,9},{14,12},{15,13},{18,16},{19,... | collective-permute-start | bytes 196616 | tf_op jit(solution)/shard_map/ppermute | solution.py:26
  80.4 0.5 collective-permute-done.5
  80.9 4.3 %collective-permute-done.4 = f32[4,4,1,1024]{3,2,1,0:T(1,128)S(1)} collective-permute-done((f32[4,4,1,1024]{3,2,1,0:T(1,128)S(1)}, f32[4,4,1,1024]{3,2,1,0:T(1,128)S(1)}, u32[]{:S(2)}, u32[]{:S(2)}) %collective-permute-start.4) | collective-permute-done | bytes 65568 | tf_op jit(solution)/shard_map/ppermute | solution.py:26
  85.5 0.8 fusion.25
  86.6 0.5 fusion.2
  87.1 0.4 fusion.60
  87.6 1.6 %collective-permute-start.7 = (f32[4,4,1,1024]{3,2,1,0:T(1,128)S(1)}, f32[4,4,1,1024]{3,2,1,0:T(1,128)S(1)}, u32[]{:S(2)}, u32[]{:S(2)}) collective-permute-start(f32[4,4,1,1024]{3,2,1,0:T(1,128)S(1)} %get-tuple-element.72), channel_id=1, source_target_pairs={{0,2},{1,3},{4,6},{5,7},{8,10},{9,11},{12,14},{13,15},{16,18},{17,... | collective-permute-start | bytes 196616 | tf_op jit(solution)/shard_map/ppermute | solution.py:25
  89.2 1.3 %collective-permute-start.6 = (f32[4,4,1,1024]{3,2,1,0:T(1,128)S(1)}, f32[4,4,1,1024]{3,2,1,0:T(1,128)S(1)}, u32[]{:S(2)}, u32[]{:S(2)}) collective-permute-start(f32[4,4,1,1024]{3,2,1,0:T(1,128)S(1)} %get-tuple-element.73), channel_id=1, source_target_pairs={{2,0},{3,1},{6,4},{7,5},{10,8},{11,9},{14,12},{15,13},{18,16},{19,... | collective-permute-start | bytes 196616 | tf_op jit(solution)/shard_map/ppermute | solution.py:26
  90.6 0.5 collective-permute-done.7
  91.1 4.3 %collective-permute-done.6 = f32[4,4,1,1024]{3,2,1,0:T(1,128)S(1)} collective-permute-done((f32[4,4,1,1024]{3,2,1,0:T(1,128)S(1)}, f32[4,4,1,1024]{3,2,1,0:T(1,128)S(1)}, u32[]{:S(2)}, u32[]{:S(2)}) %collective-permute-start.6) | collective-permute-done | bytes 65568 | tf_op jit(solution)/shard_map/ppermute | solution.py:26
  95.7 0.8 fusion.23
  96.8 0.6 fusion.3
  97.4 0.4 fusion.57
  97.9 1.6 %collective-permute-start.9 = (f32[4,4,1,1024]{3,2,1,0:T(1,128)S(1)}, f32[4,4,1,1024]{3,2,1,0:T(1,128)S(1)}, u32[]{:S(2)}, u32[]{:S(2)}) collective-permute-start(f32[4,4,1,1024]{3,2,1,0:T(1,128)S(1)} %get-tuple-element.66), channel_id=1, source_target_pairs={{0,2},{1,3},{4,6},{5,7},{8,10},{9,11},{12,14},{13,15},{16,18},{17,... | collective-permute-start | bytes 196616 | tf_op jit(solution)/shard_map/ppermute | solution.py:25
  99.5 1.5 %collective-permute-start.8 = (f32[4,4,1,1024]{3,2,1,0:T(1,128)S(1)}, f32[4,4,1,1024]{3,2,1,0:T(1,128)S(1)}, u32[]{:S(2)}, u32[]{:S(2)}) collective-permute-start(f32[4,4,1,1024]{3,2,1,0:T(1,128)S(1)} %get-tuple-element.67), channel_id=1, source_target_pairs={{2,0},{3,1},{6,4},{7,5},{10,8},{11,9},{14,12},{15,13},{18,16},{19,... | collective-permute-start | bytes 196616 | tf_op jit(solution)/shard_map/ppermute | solution.py:26
  101.4 4.3 %collective-permute-done.8 = f32[4,4,1,1024]{3,2,1,0:T(1,128)S(1)} collective-permute-done((f32[4,4,1,1024]{3,2,1,0:T(1,128)S(1)}, f32[4,4,1,1024]{3,2,1,0:T(1,128)S(1)}, u32[]{:S(2)}, u32[]{:S(2)}) %collective-permute-start.8) | collective-permute-done | bytes 65568 | tf_op jit(solution)/shard_map/ppermute | solution.py:26
  106.0 0.8 fusion.21
  107.2 0.7 fusion.4
  107.9 0.4 fusion.54
  108.4 1.6 %collective-permute-start.11 = (f32[4,4,1,1024]{3,2,1,0:T(1,128)S(1)}, f32[4,4,1,1024]{3,2,1,0:T(1,128)S(1)}, u32[]{:S(2)}, u32[]{:S(2)}) collective-permute-start(f32[4,4,1,1024]{3,2,1,0:T(1,128)S(1)} %get-tuple-element.60), channel_id=1, source_target_pairs={{0,2},{1,3},{4,6},{5,7},{8,10},{9,11},{12,14},{13,15},{16,18},{17,... | collective-permute-start | bytes 196616 | tf_op jit(solution)/shard_map/ppermute | solution.py:25
  110.0 1.3 %collective-permute-start.10 = (f32[4,4,1,1024]{3,2,1,0:T(1,128)S(1)}, f32[4,4,1,1024]{3,2,1,0:T(1,128)S(1)}, u32[]{:S(2)}, u32[]{:S(2)}) collective-permute-start(f32[4,4,1,1024]{3,2,1,0:T(1,128)S(1)} %get-tuple-element.61), channel_id=1, source_target_pairs={{2,0},{3,1},{6,4},{7,5},{10,8},{11,9},{14,12},{15,13},{18,16},{19,... | collective-permute-start | bytes 196616 | tf_op jit(solution)/shard_map/ppermute | solution.py:26
  111.4 0.5 collective-permute-done.11
  111.9 4.3 %collective-permute-done.10 = f32[4,4,1,1024]{3,2,1,0:T(1,128)S(1)} collective-permute-done((f32[4,4,1,1024]{3,2,1,0:T(1,128)S(1)}, f32[4,4,1,1024]{3,2,1,0:T(1,128)S(1)}, u32[]{:S(2)}, u32[]{:S(2)}) %collective-permute-start.10) | collective-permute-done | bytes 65568 | tf_op jit(solution)/shard_map/ppermute | solution.py:26
  116.5 0.8 fusion.19
  117.3 0.3 fusion.31
  117.6 1.7 %fusion.5 = f32[4,4,16,1024]{3,2,1,0:T(8,128)} fusion(f32[4,1,16,1024]{3,2,1,0:T(8,128)S(1)} %get-tuple-element.34, f32[4,1,16,1024]{3,2,1,0:T(8,128)S(1)} %get-tuple-element.33, f32[4,1,16,1024]{3,2,1,0:T(8,128)S(1)} %get-tuple-element.32, f32[4,1,16,1024]{3,2,1,0:T(8,128)S(1)} %get-tuple-element.35, f32[4,1,16,1024]{3,2,1,0:T(8,128)S(1)} %get-tuple-element.38, ...), kind=kLoop, calls=%fused_computation.35 | loop fusion | flops 7864320 | bytes 8388608 | tf_op jit(solution)/shard_map/add | solution.py:46
  (37 shorter events, 4.8 us)
Async XLA Ops:
  6.5 13.2 %copy-start = (f32[4,4,16,1024]{3,2,1,0:T(8,128)S(1)}, f32[4,4,16,1024]{3,2,1,0:T(8,128)}, u32[]{:S(2)}) copy-start(f32[4,4,16,1024]{3,2,1,0:T(8,128)} %param.3) | copy-start | bytes 3145732
  6.5 53.0 %all-reduce.3.cloned.1.call-start = ((), (), s32[]{:S(2)}) async-start(), calls=%async_computation | async-start | bytes 786432 | tf_op jit(solution)/shard_map/psum | solution.py:15
  8.6 11.7 %collective-permute-start.1 = (f32[4,4,1,1024]{3,2,1,0:T(1,128)}, f32[4,4,1,1024]{3,2,1,0:T(1,128)S(1)}, u32[]{:S(2)}, u32[]{:S(2)}) collective-permute-start(f32[4,4,1,1024]{3,2,1,0:T(1,128)} %get-tuple-element.90), channel_id=1, source_target_pairs={{0,2},{1,3},{4,6},{5,7},{8,10},{9,11},{12,14},{13,15},{16,18},{17,... | collective-permute-start | bytes 196616 | tf_op jit(solution)/shard_map/ppermute | solution.py:25
  13.4 6.9 %collective-permute-start = (f32[4,4,1,1024]{3,2,1,0:T(1,128)}, f32[4,4,1,1024]{3,2,1,0:T(1,128)S(1)}, u32[]{:S(2)}, u32[]{:S(2)}) collective-permute-start(f32[4,4,1,1024]{3,2,1,0:T(1,128)} %get-tuple-element.91), channel_id=1, source_target_pairs={{2,0},{3,1},{6,4},{7,5},{10,8},{11,9},{14,12},{15,13},{18,16},{19,... | collective-permute-start | bytes 196616 | tf_op jit(solution)/shard_map/ppermute | solution.py:26
  63.3 1.2 copy-start.1
  65.6 5.2 %collective-permute-start.3 = (f32[4,4,1,1024]{3,2,1,0:T(1,128)S(1)}, f32[4,4,1,1024]{3,2,1,0:T(1,128)S(1)}, u32[]{:S(2)}, u32[]{:S(2)}) collective-permute-start(f32[4,4,1,1024]{3,2,1,0:T(1,128)S(1)} %get-tuple-element.84), channel_id=1, source_target_pairs={{0,2},{1,3},{4,6},{5,7},{8,10},{9,11},{12,14},{13,15},{16,18},{17,... | collective-permute-start | bytes 196616 | tf_op jit(solution)/shard_map/ppermute | solution.py:25
  68.9 6.2 %collective-permute-start.2 = (f32[4,4,1,1024]{3,2,1,0:T(1,128)S(1)}, f32[4,4,1,1024]{3,2,1,0:T(1,128)S(1)}, u32[]{:S(2)}, u32[]{:S(2)}) collective-permute-start(f32[4,4,1,1024]{3,2,1,0:T(1,128)S(1)} %get-tuple-element.85), channel_id=1, source_target_pairs={{2,0},{3,1},{6,4},{7,5},{10,8},{11,9},{14,12},{15,13},{18,16},{19,... | collective-permute-start | bytes 196616 | tf_op jit(solution)/shard_map/ppermute | solution.py:26
  77.4 3.5 %collective-permute-start.5 = (f32[4,4,1,1024]{3,2,1,0:T(1,128)S(1)}, f32[4,4,1,1024]{3,2,1,0:T(1,128)S(1)}, u32[]{:S(2)}, u32[]{:S(2)}) collective-permute-start(f32[4,4,1,1024]{3,2,1,0:T(1,128)S(1)} %get-tuple-element.78), channel_id=1, source_target_pairs={{0,2},{1,3},{4,6},{5,7},{8,10},{9,11},{12,14},{13,15},{16,18},{17,... | collective-permute-start | bytes 196616 | tf_op jit(solution)/shard_map/ppermute | solution.py:25
  79.0 6.2 %collective-permute-start.4 = (f32[4,4,1,1024]{3,2,1,0:T(1,128)S(1)}, f32[4,4,1,1024]{3,2,1,0:T(1,128)S(1)}, u32[]{:S(2)}, u32[]{:S(2)}) collective-permute-start(f32[4,4,1,1024]{3,2,1,0:T(1,128)S(1)} %get-tuple-element.79), channel_id=1, source_target_pairs={{2,0},{3,1},{6,4},{7,5},{10,8},{11,9},{14,12},{15,13},{18,16},{19,... | collective-permute-start | bytes 196616 | tf_op jit(solution)/shard_map/ppermute | solution.py:26
  87.6 3.5 %collective-permute-start.7 = (f32[4,4,1,1024]{3,2,1,0:T(1,128)S(1)}, f32[4,4,1,1024]{3,2,1,0:T(1,128)S(1)}, u32[]{:S(2)}, u32[]{:S(2)}) collective-permute-start(f32[4,4,1,1024]{3,2,1,0:T(1,128)S(1)} %get-tuple-element.72), channel_id=1, source_target_pairs={{0,2},{1,3},{4,6},{5,7},{8,10},{9,11},{12,14},{13,15},{16,18},{17,... | collective-permute-start | bytes 196616 | tf_op jit(solution)/shard_map/ppermute | solution.py:25
  89.2 6.2 %collective-permute-start.6 = (f32[4,4,1,1024]{3,2,1,0:T(1,128)S(1)}, f32[4,4,1,1024]{3,2,1,0:T(1,128)S(1)}, u32[]{:S(2)}, u32[]{:S(2)}) collective-permute-start(f32[4,4,1,1024]{3,2,1,0:T(1,128)S(1)} %get-tuple-element.73), channel_id=1, source_target_pairs={{2,0},{3,1},{6,4},{7,5},{10,8},{11,9},{14,12},{15,13},{18,16},{19,... | collective-permute-start | bytes 196616 | tf_op jit(solution)/shard_map/ppermute | solution.py:26
  97.9 3.5 %collective-permute-start.9 = (f32[4,4,1,1024]{3,2,1,0:T(1,128)S(1)}, f32[4,4,1,1024]{3,2,1,0:T(1,128)S(1)}, u32[]{:S(2)}, u32[]{:S(2)}) collective-permute-start(f32[4,4,1,1024]{3,2,1,0:T(1,128)S(1)} %get-tuple-element.66), channel_id=1, source_target_pairs={{0,2},{1,3},{4,6},{5,7},{8,10},{9,11},{12,14},{13,15},{16,18},{17,... | collective-permute-start | bytes 196616 | tf_op jit(solution)/shard_map/ppermute | solution.py:25
  99.5 6.2 %collective-permute-start.8 = (f32[4,4,1,1024]{3,2,1,0:T(1,128)S(1)}, f32[4,4,1,1024]{3,2,1,0:T(1,128)S(1)}, u32[]{:S(2)}, u32[]{:S(2)}) collective-permute-start(f32[4,4,1,1024]{3,2,1,0:T(1,128)S(1)} %get-tuple-element.67), channel_id=1, source_target_pairs={{2,0},{3,1},{6,4},{7,5},{10,8},{11,9},{14,12},{15,13},{18,16},{19,... | collective-permute-start | bytes 196616 | tf_op jit(solution)/shard_map/ppermute | solution.py:26
  108.4 3.5 %collective-permute-start.11 = (f32[4,4,1,1024]{3,2,1,0:T(1,128)S(1)}, f32[4,4,1,1024]{3,2,1,0:T(1,128)S(1)}, u32[]{:S(2)}, u32[]{:S(2)}) collective-permute-start(f32[4,4,1,1024]{3,2,1,0:T(1,128)S(1)} %get-tuple-element.60), channel_id=1, source_target_pairs={{0,2},{1,3},{4,6},{5,7},{8,10},{9,11},{12,14},{13,15},{16,18},{17,... | collective-permute-start | bytes 196616 | tf_op jit(solution)/shard_map/ppermute | solution.py:25
  110.0 6.2 %collective-permute-start.10 = (f32[4,4,1,1024]{3,2,1,0:T(1,128)S(1)}, f32[4,4,1,1024]{3,2,1,0:T(1,128)S(1)}, u32[]{:S(2)}, u32[]{:S(2)}) collective-permute-start(f32[4,4,1,1024]{3,2,1,0:T(1,128)S(1)} %get-tuple-element.61), channel_id=1, source_target_pairs={{2,0},{3,1},{6,4},{7,5},{10,8},{11,9},{14,12},{15,13},{18,16},{19,... | collective-permute-start | bytes 196616 | tf_op jit(solution)/shard_map/ppermute | solution.py:26
Sparse Core Ops, SparseCore 0:
  19.8 39.6 all-reduce.2
where the time goes:
time: 127 us; the launch traced here: 126 us
  waiting for transfers between devices  61.6 us (49%)
  starting transfers between devices  22.4 us (18%)
  other arithmetic  16.8 us (13%)
  between operations  15.7 us (12%)
  local copies, waits for them, and re-layouts  7.19 us (6%)
  blocking collectives  2.37 us (2%)
    psum x1, waiting for transfers between devices, broadcast(): return lax.psum(kept, axis)  38 us
    ppermute x6, waiting for transfers between devices, padded_2(): after = lax.ppermute(first, axis, down)  21.4 us
    ppermute x6, starting transfers between devices, padded_2(): before = lax.ppermute(last, axis, up)  14.5 us
    ppermute x6, starting transfers between devices, padded_2(): after = lax.ppermute(first, axis, down)  7.93 us
    mul x6, other arithmetic, advance(): grad_x = (east - west) * 0.5  4.97 us
    add x6, other arithmetic, advance(): centre + time_step * jnp.stack([height, zonal, merid, tracer], axis=-3)  3.97 us
    slice x12, local copies, waits for them, and re-layouts, advance(): east = jnp.roll(centre, -1, axis=-1)  2.86 us
    mul x6, other arithmetic, advance(): grad_y = (north - south) * 0.5  2.83 us
  transfers between devices with their start and end apart: 13, of which 11 were waited for; matrix products, arithmetic and copies ran while one was open for 4% of the time, Pallas kernels for 0%

commit v1 on v0

v1 whole, which is shorter than its diff:
```python
import functools

import jax
import jax.numpy as jnp
import numpy as np
from jax import lax
from jax.experimental import pallas as pl
from jax.experimental.pallas import tpu as pltpu
from jax.sharding import PartitionSpec as P

STEPS = 6
MESH = pl.DeviceIdType.MESH
SUB = 8
CHUNKS = 4
CAPS = (1, 3, 5, 5)


def kernel(n, nlat, mem, rows, owners_ref, perturb_ref, traj_ref, out_ref,
           vin, tin, vout, state, rec, cor, own, *rest):
    gather = rest[:CHUNKS]
    (in_sem, out_sem, zsend, zrecv, csend, crecv, fsend, hsend, hrecv) = rest[CHUNKS:]
    z = lax.axis_index("pert")
    core = lax.axis_index("fld")
    lat = lax.axis_index("lat")
    other = 1 - core
    even = lat % 2 == 0
    near = jnp.where(even, lat + 1, lat - 1)
    far = jnp.where(even, lat - 1, lat + 1)
    has_near = near < nlat
    has_far = jnp.logical_and(far >= 0, far < nlat)
    span = rows // CHUNKS
    fields = 4
    mf = mem * fields
    wide = mf * SUB

    def phys(q):
        return jnp.where(even, rows - 1 - q, q)

    def line(s, r):
        return pl.multiple_of(((s * (rows + 2)) + r + 1) * wide, wide)

    def first_row(k):
        return jnp.where(even, rows - (k + 1) * span, k * span)

    t_in = pltpu.make_async_copy(traj_ref.at[0], tin, in_sem.at[0])
    t_in.start()
    s_in = pltpu.make_async_copy(perturb_ref, vin, in_sem.at[1])
    s_in.start()

    barrier = pltpu.get_barrier_semaphore()
    for t in range(n):
        @pl.when(z != t)
        def _():
            pl.semaphore_signal(barrier, inc=1, device_id={"pert": t}, device_id_type=MESH)
    pl.semaphore_signal(barrier, inc=1, device_id={"fld": other}, device_id_type=MESH)

    @pl.when(has_near)
    def _():
        pl.semaphore_signal(barrier, inc=1, device_id={"lat": near}, device_id_type=MESH)
    if nlat > 2:
        @pl.when(has_far)
        def _():
            pl.semaphore_signal(barrier, inc=1, device_id={"lat": far}, device_id_type=MESH)

    block = span * 2

    def piece(k, slot, half):
        return gather[k].at[pl.ds((slot * 2 + half) * block, block)]

    t_in.wait()
    halves = rows // SUB
    for f in range(2):
        for g in range(halves):
            for j in range(8):
                own[pl.ds((g * SUB * 2 + f) * SUB + j, SUB, stride=2 * SUB), :] = (
                    tin[f, g * SUB:(g + 1) * SUB, j * 128:(j + 1) * 128])
    for k in range(CHUNKS):
        for i in range(span * 2):
            at = (z * 2 + core) * block + i
            src = pl.multiple_of(first_row(k) * 2 * SUB, SUB) + i * SUB
            gather[k][at] = own[pl.ds(src, SUB), :]

    amount = n - 1 + 1 + jnp.where(has_near, 1, 0)
    if nlat > 2:
        amount = amount + jnp.where(has_far, 1, 0)
    pl.semaphore_wait(barrier, amount)

    def z_copy(k, target):
        own = piece(k, z, core)
        return pltpu.make_async_remote_copy(
            src_ref=own, dst_ref=own, send_sem=zsend.at[k, target], recv_sem=zrecv.at[k, z],
            device_id={"pert": target}, device_id_type=MESH)

    def z_arrival(k, slot):
        there = piece(k, slot, core)
        return pltpu.make_async_remote_copy(
            src_ref=there, dst_ref=there, send_sem=zsend.at[k, slot], recv_sem=zrecv.at[k, slot],
            device_id={"pert": slot}, device_id_type=MESH)

    def relay(k, slot, target):
        there = piece(k, slot, core)
        return pltpu.make_async_remote_copy(
            src_ref=there, dst_ref=there, send_sem=fsend.at[k], recv_sem=zrecv.at[k, slot],
            device_id={"pert": target}, device_id_type=MESH)

    def c_copy(k, slot):
        there = piece(k, slot, core)
        return pltpu.make_async_remote_copy(
            src_ref=there, dst_ref=there, send_sem=csend.at[k, slot], recv_sem=crecv.at[k, slot],
            device_id={"fld": other}, device_id_type=MESH)

    def c_arrival(k, slot):
        there = piece(k, slot, other)
        return pltpu.make_async_remote_copy(
            src_ref=there, dst_ref=there, send_sem=csend.at[k, slot], recv_sem=crecv.at[k, slot],
            device_id={"fld": other}, device_id_type=MESH)

    def direct(target):
        ok = z != target
        if n == 4 and target in (0, 3):
            ok = jnp.logical_and(ok, z != 3 - target)
        return ok

    for k in range(CHUNKS):
        for t in range(n):
            @pl.when(direct(t))
            def _():
                z_copy(k, t).start()
        c_copy(k, z).start()

    s_in.wait()
    zero = jnp.zeros((SUB, 128), jnp.float32)

    def relayout_in(g, i):
        for j in range(8):
            x = vin[i, pl.ds(pl.multiple_of(g * SUB, SUB), SUB), j * 128:(j + 1) * 128]
            state[pl.ds(line(0, g * SUB) + i * SUB + j, SUB, stride=wide), :] = x

    def halo(s, side):
        q = 0 if side == 0 else rows - 1
        r = phys(q)
        beyond = phys(-1 if side == 0 else rows)
        partner = near if side == 0 else far
        there = rows - 1 - beyond
        return pltpu.make_async_remote_copy(
            src_ref=state.at[pl.ds(line(s, r), wide), :],
            dst_ref=state.at[pl.ds(line(s, there), wide), :],
            send_sem=hsend.at[s, side], recv_sem=hrecv.at[s, side],
            device_id={"lat": partner}, device_id_type=MESH)

    def halo_arrival(s, side):
        beyond = phys(-1 if side == 0 else rows)
        here = state.at[pl.ds(line(s, beyond), wide), :]
        partner = near if side == 0 else far
        return pltpu.make_async_remote_copy(
            src_ref=here, dst_ref=here, send_sem=hsend.at[s, side], recv_sem=hrecv.at[s, side],
            device_id={"lat": partner}, device_id_type=MESH)

    near_group = jnp.where(even, halves - 1, 0)

    @pl.loop(0, mf)
    def _(i):
        relayout_in(near_group, i)

    @pl.when(has_near)
    def _():
        halo(0, 0).start()

    for g in range(1, halves):
        @pl.loop(0, mf)
        def _(i):
            relayout_in(jnp.where(even, halves - 1 - g, g), i)

    if nlat > 2:
        @pl.when(has_far)
        def _():
            halo(0, 1).start()

    def clear(q):
        @pl.loop(0, STEPS)
        def _(s):
            @pl.loop(0, mf)
            def _(i):
                state[pl.ds(line(s, phys(q)) + pl.multiple_of(i * SUB, SUB), SUB), :] = zero

    @pl.when(jnp.logical_not(has_near))
    def _():
        clear(-1)

    @pl.when(jnp.logical_not(has_far))
    def _():
        clear(rows)

    total = rows * nlat

    @pl.loop(0, rows)
    def _(r):
        number = jnp.full((SUB, 128), lat * rows + r, jnp.int32).astype(jnp.float32)
        cor[pl.ds(pl.multiple_of(r * SUB, SUB), SUB), :] = 0.1 * jnp.sin(
            jnp.float32(np.pi) * ((number + 0.5) / total - 0.5))

    lane = lax.broadcasted_iota(jnp.int32, (SUB, 128), 1)
    at_first, at_last = lane == 0, lane == 127

    def collect(k):
        def pass_on(slot):
            z_arrival(k, slot).wait_recv()
            c_copy(k, slot).start()
        if n == 4:
            for end, via in ((3, 2), (0, 1)):
                @pl.when(z == via)
                def _():
                    pass_on(3 - end)
                    relay(k, 3 - end, end).start()
        for slot in range(n):
            fresh = z != slot
            if n == 4 and slot in (0, 3):
                fresh = jnp.logical_and(fresh, z != (2 if slot == 0 else 1))

            @pl.when(fresh)
            def _():
                pass_on(slot)
        for slot in range(n):
            c_arrival(k, slot).wait_recv()
        for record in range(3):
            slot = owners_ref[record]
            for f in range(4):
                for rr in range(span):
                    src = ((slot * 2 + f // 2) * span + rr) * 2 + f % 2
                    dst = (record * 4 + f) * rows + first_row(k) + rr
                    rec[pl.ds(pl.multiple_of(dst * SUB, SUB), SUB), :] = (
                        gather[k][src])

    def one_row(s, r):
        earlier, weight = s // 3, (s % 3) / 3.0

        def coef(f):
            at = ((earlier * 4 + f) * rows + r) * SUB
            low = rec[pl.ds(pl.multiple_of(at, SUB), SUB), :]
            if s % 3 == 0:
                return low
            at = (((earlier + 1) * 4 + f) * rows + r) * SUB
            return (1.0 - weight) * low + weight * rec[pl.ds(pl.multiple_of(at, SUB), SUB), :]

        half_u, half_v = 0.05 * coef(0), 0.05 * coef(1)
        depth, mix = 0.05 * coef(2), 0.1 * coef(3)
        to_e, to_w, to_n, to_s = mix - half_u, mix + half_u, mix - half_v, mix + half_v
        to_c = 1.0 - 4.0 * mix
        turn = cor[pl.ds(pl.multiple_of(r * SUB, SUB), SUB), :]
        c_at, n_at, s_at, o_at = line(s, r), line(s, r + 1), line(s, r - 1), line(s + 1, r)
        for m in range(mem):
            c, nn, ss, de, base = [], [], [], [], []
            for f in range(fields):
                off = (m * fields + f) * SUB
                x = state[pl.ds(c_at + off, SUB), :]
                north = state[pl.ds(n_at + off, SUB), :]
                south = state[pl.ds(s_at + off, SUB), :]
                e = pltpu.roll(x, 127, 1)
                e = jnp.where(at_last, pltpu.roll(e, SUB - 1, 0), e)
                w = pltpu.roll(x, 1, 1)
                w = jnp.where(at_first, pltpu.roll(w, 1, 0), w)
                c.append(x)
                nn.append(north)
                ss.append(south)
                de.append(e - w)
                base.append((to_c * x + to_e * e) + (to_w * w + to_n * north) + to_s * south)
            div = de[1] + (nn[2] - ss[2])
            new = (
                base[0] - depth * div,
                base[1] - 0.05 * de[0] + turn * c[2],
                base[2] - 0.05 * (nn[0] - ss[0]) - turn * c[1],
                base[3] - 0.025 * div,
            )
            for f in range(fields):
                state[pl.ds(o_at + (m * fields + f) * SUB, SUB), :] = new[f]

    done = [0] * STEPS
    for k in range(CHUNKS):
        last = k == CHUNKS - 1
        collect(k)
        for s in range(CAPS[k] + 1):
            limit = rows if last else max((k + 1) * span - s, 0)
            start = done[s]
            if limit <= start:
                continue
            if start == 0:
                @pl.when(has_near)
                def _():
                    halo_arrival(s, 0).wait_recv()
                one_row(s, phys(0))
                if s + 1 < STEPS:
                    @pl.when(has_near)
                    def _():
                        halo(s + 1, 0).start()
                start = 1
            if limit == rows and nlat > 2:
                @pl.when(has_far)
                def _():
                    halo_arrival(s, 1).wait_recv()
            if limit > start:
                @pl.loop(start, limit)
                def _(q):
                    one_row(s, phys(q))
            if limit == rows and nlat > 2 and s + 1 < STEPS:
                @pl.when(has_far)
                def _():
                    halo(s + 1, 1).start()
            done[s] = limit

    @pl.loop(0, mf)
    def _(i):
        for g in range(halves):
            for j in range(8):
                vout[i, g * SUB:(g + 1) * SUB, j * 128:(j + 1) * 128] = (
                    state[pl.ds(line(STEPS, g * SUB) + i * SUB + j, SUB, stride=wide), :])
    s_out = pltpu.make_async_copy(vout, out_ref, out_sem)
    s_out.start()

    for k in range(CHUNKS):
        for t in range(n):
            @pl.when(direct(t))
            def _():
                z_copy(k, t).wait_send()
            c_copy(k, t).wait_send()
        if n == 4:
            for end, via in ((3, 2), (0, 1)):
                @pl.when(z == via)
                def _():
                    relay(k, 3 - end, end).wait_send()
    for s in range(STEPS):
        @pl.when(has_near)
        def _():
            halo(s, 0).wait_send()
        if nlat > 2:
            @pl.when(has_far)
            def _():
                halo(s, 1).wait_send()
    s_out.wait()


def per_device(perturb, traj_store, owners):
    n, nlat = lax.axis_size("pert"), lax.axis_size("lat")
    mem, fields, rows, lon = perturb.shape
    span = rows // CHUNKS
    f32 = jnp.float32
    dma = pltpu.SemaphoreType.DMA
    out = pl.pallas_call(
        functools.partial(kernel, n, nlat, mem, rows),
        out_shape=jax.ShapeDtypeStruct((mem * fields, rows, lon), f32),
        in_specs=[pl.BlockSpec(memory_space=pltpu.SMEM),
                  pl.BlockSpec(memory_space=pl.ANY),
                  pl.BlockSpec(memory_space=pl.ANY)],
        out_specs=pl.BlockSpec(memory_space=pl.ANY),
        scratch_shapes=[
            pltpu.VMEM((mem * fields, rows, lon), f32),
            pltpu.VMEM((2, rows, lon), f32),
            pltpu.VMEM((mem * fields, rows, lon), f32),
            pltpu.VMEM(((STEPS + 1) * (rows + 2) * mem * fields * SUB, 128), f32),
            pltpu.VMEM((3 * 4 * rows * SUB, 128), f32),
            pltpu.VMEM((rows * SUB, 128), f32),
            pltpu.VMEM((rows * 2 * SUB, 128), f32),
            *[pltpu.VMEM((n * 2 * span * 2, SUB, 128), f32) for _ in range(CHUNKS)],
            dma((2,)), dma(()),
            dma((CHUNKS, n)), dma((CHUNKS, n)), dma((CHUNKS, n)), dma((CHUNKS, n)),
            dma((CHUNKS,)), dma((STEPS, 2)), dma((STEPS, 2)),
        ],
        compiler_params=pltpu.CompilerParams(
            collective_id=0, has_side_effects=True, vmem_limit_bytes=48 * 2**20),
    )(owners, perturb.reshape(mem * fields, rows, lon), traj_store)
    return out.reshape(mem, fields, rows, lon)


def solution(mesh):
    in_specs = (
        P(("groups", "pert", "fld"), None, "lat", None),
        P(("groups", "pert"), "fld", "lat", None),
        P("groups"),
    )
    out_specs = P(("groups", "pert", "fld"), None, "lat", None)
    return jax.shard_map(
        per_device, mesh=mesh, in_specs=in_specs, out_specs=out_specs, check_vma=False
    )
```

time: 127 us -> 42.8 us (0.34)
  the two profiles are of different devices: /device:TPU:0 before, /device:TPU:1 now
where the time goes in v1:
time: 42.8 us; the launch traced here: 42.6 us
  Pallas kernels  38.9 us (91%)
  local copies, waits for them, and re-layouts  3.76 us (9%)
    pallas_call x1, Pallas kernels, per_device(): pl.pallas_call(functools.partial(kernel, n, nlat, mem, rows), out_shape=j...  38.9 us
    unnamed x7, local copies, waits for them, and re-layouts  3.76 us

profile of v1, /device:TPU:1, one launch (start us, length us, event | category | flops | bytes accessed | tf_op | source)
XLA Modules:
  0.0 42.6 jit_solution(10779478916727840009)
XLA Ops:
  0.0 0.0 copy-start.2
  0.0 0.7 %copy-done.2 = s32[3]{0:T(128)S(1)} copy-done((s32[3]{0:T(128)S(1)}, s32[3]{0:T(128)}, u32[]{:S(2)}) %copy-start.2) | copy-done | bytes 36
  0.7 0.0 copy-start
  0.7 1.2 %copy-done = f32[4,4,16,1024]{3,2,1,0:T(8,128)S(1)} copy-done((f32[4,4,16,1024]{3,2,1,0:T(8,128)S(1)}, f32[4,4,16,1024]{3,2,1,0:T(8,128)}, u32[]{:S(2)}) %copy-start) | copy-done | bytes 1048600
  1.9 0.0 copy-start.1
  1.9 0.9 %copy-done.1 = f32[1,2,16,1024]{3,2,1,0:T(8,128)S(1)} copy-done((f32[1,2,16,1024]{3,2,1,0:T(8,128)S(1)}, f32[1,2,16,1024]{3,2,1,0:T(8,128)}, u32[]{:S(2)}) %copy-start.1) | copy-done | bytes 131096
  2.8 38.9 %shard_map.37 = f32[16,16,1024]{2,1,0:T(8,128)S(1)} custom-call(s32[3]{0:T(128)S(1)} %copy-done.2, f32[16,16,1024]{2,1,0:T(8,128)S(1)} %bitcast.3, f32[1,2,16,1024]{3,2,1,0:T(8,128)S(1)} %copy-done.1), custom_call_target="tpu_custom_call" | custom-call | tf_op jit(solution)/shard_map/pallas_call | solution.py:347
  41.7 1.0 %copy.5 = f32[4,4,16,1024]{3,2,1,0:T(8,128)} copy(f32[4,4,16,1024]{3,2,1,0:T(8,128)S(1)} %bitcast.2) | data formatting | bytes 2097152
Async XLA Ops:
  0.0 0.7 %copy-start.2 = (s32[3]{0:T(128)S(1)}, s32[3]{0:T(128)}, u32[]{:S(2)}) copy-start(s32[3]{0:T(128)} %owners_ref.1) | copy-start | bytes 40
  0.7 1.2 %copy-start = (f32[4,4,16,1024]{3,2,1,0:T(8,128)S(1)}, f32[4,4,16,1024]{3,2,1,0:T(8,128)}, u32[]{:S(2)}) copy-start(f32[4,4,16,1024]{3,2,1,0:T(8,128)} %param.3) | copy-start | bytes 3145732
  1.9 0.9 %copy-start.1 = (f32[1,2,16,1024]{3,2,1,0:T(8,128)S(1)}, f32[1,2,16,1024]{3,2,1,0:T(8,128)}, u32[]{:S(2)}) copy-start(f32[1,2,16,1024]{3,2,1,0:T(8,128)} %traj_ref.1) | copy-start | bytes 393220

commit v2 on v1

v2 whole, which is shorter than its diff:
```python
import functools

import jax
import jax.numpy as jnp
import numpy as np
from jax import lax
from jax.experimental import pallas as pl
from jax.experimental.pallas import tpu as pltpu
from jax.sharding import PartitionSpec as P

STEPS = 6
MESH = pl.DeviceIdType.MESH
SUB = 8
SPAN = 4
PAIR = 2


def chunk_plan(nlat, rows, reach):
    plan = [("far", rows, rows + reach)] if nlat > 2 else []
    plan += [("own", q, q + SPAN) for q in range(rows - SPAN, -1, -SPAN)]
    return plan + [("near", -reach, 0)]


def kernel(n, nlat, mem, rows, plan, owners_ref, perturb_ref, traj_ref, out_ref,
           vin, tin, vout, rec, cor, own, *rest):
    state, rest = rest[:STEPS + 1], rest[STEPS + 1:]
    count = len(plan)
    gather = rest[:count]
    (in_sem, out_sem, zsend, zrecv, csend, crecv, fsend,
     hsend, hrecv, bsend, brecv) = rest[count:]
    z = lax.axis_index("pert")
    core = lax.axis_index("fld")
    lat = lax.axis_index("lat")
    other = 1 - core
    even = lat % 2 == 0
    near = jnp.where(even, lat + 1, lat - 1)
    far = jnp.where(even, lat - 1, lat + 1)
    has_near = near < nlat
    has_far = jnp.logical_and(far >= 0, far < nlat)
    fields = 4
    mf = mem * fields
    wide = mf * SUB
    reach = STEPS - 1
    halves = rows // SUB
    sides = {"near": (0, near, has_near), "far": (1, far, has_far)}
    if nlat <= 2:
        del sides["far"]

    def guarded(kind):
        def run(body):
            if kind == "own":
                body()
            else:
                pl.when(sides[kind][2])(body)
        return run

    def phys(q):
        return jnp.where(even, rows - 1 - q, q)

    def line(r):
        return pl.multiple_of((r + STEPS) * wide, wide)

    def start_of(k):
        _, q0, q1 = plan[k]
        return jnp.where(even, rows - q1, q0)

    t_in = pltpu.make_async_copy(traj_ref.at[0], tin, in_sem.at[0])
    t_in.start()
    s_in = pltpu.make_async_copy(perturb_ref, vin, in_sem.at[1])
    s_in.start()

    barrier = pltpu.get_barrier_semaphore()
    for t in range(n):
        @pl.when(z != t)
        def _():
            pl.semaphore_signal(barrier, inc=1, device_id={"pert": t}, device_id_type=MESH)
    pl.semaphore_signal(barrier, inc=1, device_id={"fld": other}, device_id_type=MESH)
    amount = n - 1 + 1
    for kind, (_, partner, present) in sides.items():
        @pl.when(present)
        def _():
            pl.semaphore_signal(barrier, inc=1, device_id={"lat": partner}, device_id_type=MESH)
        amount = amount + jnp.where(present, 1, 0)

    def piece(k, slot, half):
        block = (plan[k][2] - plan[k][1]) * 2
        return gather[k].at[pl.ds((slot * 2 + half) * block, block)]

    t_in.wait()
    for f in range(2):
        for g in range(halves):
            for j in range(8):
                own[pl.ds((g * SUB * 2 + f) * SUB + j, SUB, stride=2 * SUB), :] = (
                    tin[f, g * SUB:(g + 1) * SUB, j * 128:(j + 1) * 128])
    whole = own.reshape(rows * 2, SUB, 128)
    for k, (kind, q0, q1) in enumerate(plan):
        if kind != "own":
            continue
        block = (q1 - q0) * 2
        for i in range(block):
            src = pl.multiple_of((start_of(k) * 2 + i) * SUB, SUB)
            gather[k][(z * 2 + core) * block + i] = own[pl.ds(src, SUB), :]

    pl.semaphore_wait(barrier, amount)

    def border(kind, k):
        side, partner, _ = sides[kind]
        src = jnp.where(partner > lat, rows - reach, 0)
        return pltpu.make_async_remote_copy(
            src_ref=whole.at[pl.ds(src * 2, reach * 2)], dst_ref=piece(k, z, core),
            send_sem=bsend.at[side], recv_sem=brecv.at[side],
            device_id={"lat": partner}, device_id_type=MESH)

    def z_copy(k, target):
        mine = piece(k, z, core)
        return pltpu.make_async_remote_copy(
            src_ref=mine, dst_ref=mine, send_sem=zsend.at[k, target], recv_sem=zrecv.at[k, z],
            device_id={"pert": target}, device_id_type=MESH)

    def z_arrival(k, slot):
        there = piece(k, slot, core)
        return pltpu.make_async_remote_copy(
            src_ref=there, dst_ref=there, send_sem=zsend.at[k, slot], recv_sem=zrecv.at[k, slot],
            device_id={"pert": slot}, device_id_type=MESH)

    def relay(k, slot, target):
        there = piece(k, slot, core)
        return pltpu.make_async_remote_copy(
            src_ref=there, dst_ref=there, send_sem=fsend.at[k], recv_sem=zrecv.at[k, slot],
            device_id={"pert": target}, device_id_type=MESH)

    def c_copy(k, slot):
        there = piece(k, slot, core)
        return pltpu.make_async_remote_copy(
            src_ref=there, dst_ref=there, send_sem=csend.at[k, slot], recv_sem=crecv.at[k, slot],
            device_id={"fld": other}, device_id_type=MESH)

    def c_arrival(k, slot):
        there = piece(k, slot, other)
        return pltpu.make_async_remote_copy(
            src_ref=there, dst_ref=there, send_sem=csend.at[k, slot], recv_sem=crecv.at[k, slot],
            device_id={"fld": other}, device_id_type=MESH)

    def direct(target):
        ok = z != target
        if n == 4 and target in (0, 3):
            ok = jnp.logical_and(ok, z != 3 - target)
        return ok

    def send_out(k):
        for t in range(n):
            @pl.when(direct(t))
            def _():
                z_copy(k, t).start()
        c_copy(k, z).start()

    for k, (kind, _, _) in enumerate(plan):
        if kind != "own":
            @guarded(kind)
            def _():
                border(kind, k).start()
    for k, (kind, _, _) in enumerate(plan):
        if kind == "own":
            send_out(k)

    s_in.wait()
    zero = jnp.zeros((SUB, 128), jnp.float32)

    @pl.loop(0, mf)
    def _(i):
        for g in range(halves):
            for j in range(8):
                x = vin[i, g * SUB:(g + 1) * SUB, j * 128:(j + 1) * 128]
                state[0][pl.ds(line(g * SUB) + i * SUB + j, SUB, stride=wide), :] = x

    def halo(kind):
        side, partner, _ = sides[kind]
        src = jnp.where(partner > lat, rows - STEPS, 0)
        dst = jnp.where(partner > lat, -STEPS, rows)
        return pltpu.make_async_remote_copy(
            src_ref=state[0].at[pl.ds(line(src), STEPS * wide), :],
            dst_ref=state[0].at[pl.ds(line(dst), STEPS * wide), :],
            send_sem=hsend.at[side], recv_sem=hrecv.at[side],
            device_id={"lat": partner}, device_id_type=MESH)

    def halo_arrival(kind):
        side, partner, _ = sides[kind]
        here = state[0].at[pl.ds(line(jnp.where(partner > lat, rows, -STEPS)), STEPS * wide), :]
        return pltpu.make_async_remote_copy(
            src_ref=here, dst_ref=here, send_sem=hsend.at[side], recv_sem=hrecv.at[side],
            device_id={"lat": partner}, device_id_type=MESH)

    for k, (kind, _, _) in enumerate(plan):
        if kind != "own":
            @guarded(kind)
            def _():
                halo(kind).start()
                border(kind, k).wait_recv()
                send_out(k)

    def clear(q):
        for s in range(STEPS):
            @pl.loop(0, mf)
            def _(i):
                state[s][pl.ds(line(phys(q)) + pl.multiple_of(i * SUB, SUB), SUB), :] = zero

    @pl.when(jnp.logical_not(has_near))
    def _():
        clear(-1)

    @pl.when(jnp.logical_not(has_far))
    def _():
        clear(rows)

    total = rows * nlat

    @pl.loop(0, rows + 2 * reach)
    def _(r):
        number = jnp.full((SUB, 128), lat * rows + r - reach, jnp.int32).astype(jnp.float32)
        cor[r] = 0.1 * jnp.sin(jnp.float32(np.pi) * ((number + 0.5) / total - 0.5))

    lane = lax.broadcasted_iota(jnp.int32, (SUB, 128), 1)
    at_first, at_last = lane == 0, lane == 127

    def collect(k):
        span = plan[k][2] - plan[k][1]

        def pass_on(slot):
            z_arrival(k, slot).wait_recv()
            c_copy(k, slot).start()
        if n == 4:
            for end, via in ((3, 2), (0, 1)):
                @pl.when(z == via)
                def _():
                    z_arrival(k, 3 - end).wait_recv()
                    relay(k, 3 - end, end).start()
                    c_copy(k, 3 - end).start()
        for slot in range(n):
            fresh = z != slot
            if n == 4 and slot in (0, 3):
                fresh = jnp.logical_and(fresh, z != (2 if slot == 0 else 1))

            @pl.when(fresh)
            def _():
                pass_on(slot)
        for slot in range(n):
            c_arrival(k, slot).wait_recv()
        for record in range(3):
            slot = owners_ref[record]
            for f in range(4):
                for rr in range(span):
                    src = ((slot * 2 + f // 2) * span + rr) * 2 + f % 2
                    rec[(start_of(k) + rr + reach) * 12 + record * 4 + f] = gather[k][src]

    def one_row(s, r):
        earlier, weight = s // 3, (s % 3) / 3.0

        def coef(f):
            at = (r + reach) * 12 + earlier * 4 + f
            low = rec[at]
            if s % 3 == 0:
                return low
            return (1.0 - weight) * low + weight * rec[at + 4]

        half_u, half_v = 0.05 * coef(0), 0.05 * coef(1)
        depth, mix = 0.05 * coef(2), 0.1 * coef(3)
        to_e, to_w, to_n, to_s = mix - half_u, mix + half_u, mix - half_v, mix + half_v
        to_c = 1.0 - 4.0 * mix
        turn = cor[r + reach]
        c_at, n_at, s_at = line(r), line(r + 1), line(r - 1)
        held = []

        def flush():
            for at, value in held:
                state[s + 1][pl.ds(at, SUB), :] = value
            held.clear()

        for m in range(mem):
            c, nn, ss, de, base = [], [], [], [], []
            for f in range(fields):
                off = (m * fields + f) * SUB
                x = state[s][pl.ds(c_at + off, SUB), :]
                north = state[s][pl.ds(n_at + off, SUB), :]
                south = state[s][pl.ds(s_at + off, SUB), :]
                e = pltpu.roll(x, 127, 1)
                e = jnp.where(at_last, pltpu.roll(e, SUB - 1, 0), e)
                w = pltpu.roll(x, 1, 1)
                w = jnp.where(at_first, pltpu.roll(w, 1, 0), w)
                c.append(x)
                nn.append(north)
                ss.append(south)
                de.append(e - w)
                base.append((to_c * x + to_e * e) + (to_w * w + to_n * north) + to_s * south)
            div = de[1] + (nn[2] - ss[2])
            new = (
                base[0] - depth * div,
                base[1] - 0.05 * de[0] + turn * c[2],
                base[2] - 0.05 * (nn[0] - ss[0]) - turn * c[1],
                base[3] - 0.025 * div,
            )
            flush()
            held += [(c_at + (m * fields + f) * SUB, new[f]) for f in range(fields)]
        flush()

    def rows_of(s, low, high):
        if isinstance(low, int) and isinstance(high, int):
            pairs = max(high - low, 0) // PAIR
            if pairs:
                @pl.loop(0, pairs)
                def _(p):
                    for i in range(PAIR):
                        one_row(s, phys(low + p * PAIR + i))
            for q in range(low + pairs * PAIR, high):
                one_row(s, phys(q))
        else:
            @pl.loop(low, high)
            def _(q):
                one_row(s, phys(q))

    done = [rows + (jnp.where(has_far, reach - s, 0) if nlat > 2 else 0) for s in range(STEPS)]
    for k, (kind, front, _) in enumerate(plan):
        @guarded(kind)
        def _():
            collect(k)
        if kind == "far":
            @guarded(kind)
            def _():
                halo_arrival(kind).wait_recv()
            continue
        if front == 0:
            @guarded("near")
            def _():
                halo_arrival("near").wait_recv()
        for s in range(STEPS):
            low = front + s
            if kind == "near" and nlat % 2:
                low = jnp.where(has_near, low, 0)
            elif low >= rows:
                continue
            rows_of(s, low, done[s])
            done[s] = low

    @pl.loop(0, mf)
    def _(i):
        for g in range(halves):
            for j in range(8):
                vout[i, g * SUB:(g + 1) * SUB, j * 128:(j + 1) * 128] = (
                    state[STEPS][pl.ds(line(g * SUB) + i * SUB + j, SUB, stride=wide), :])
    s_out = pltpu.make_async_copy(vout, out_ref, out_sem)
    s_out.start()

    for k, (kind, _, _) in enumerate(plan):
        @guarded(kind)
        def _():
            for t in range(n):
                @pl.when(direct(t))
                def _():
                    z_copy(k, t).wait_send()
                c_copy(k, t).wait_send()
            if n == 4:
                for end, via in ((3, 2), (0, 1)):
                    @pl.when(z == via)
                    def _():
                        relay(k, 3 - end, end).wait_send()
            if kind != "own":
                border(kind, k).wait_send()
                halo(kind).wait_send()
    s_out.wait()


def per_device(perturb, traj_store, owners):
    n, nlat = lax.axis_size("pert"), lax.axis_size("lat")
    mem, fields, rows, lon = perturb.shape
    reach = STEPS - 1
    plan = chunk_plan(nlat, rows, reach)
    f32 = jnp.float32
    dma = pltpu.SemaphoreType.DMA
    marks = dma((len(plan), n))
    out = pl.pallas_call(
        functools.partial(kernel, n, nlat, mem, rows, plan),
        out_shape=jax.ShapeDtypeStruct((mem * fields, rows, lon), f32),
        in_specs=[pl.BlockSpec(memory_space=pltpu.SMEM),
                  pl.BlockSpec(memory_space=pl.ANY),
                  pl.BlockSpec(memory_space=pl.ANY)],
        out_specs=pl.BlockSpec(memory_space=pl.ANY),
        scratch_shapes=[
            pltpu.VMEM((mem * fields, rows, lon), f32),
            pltpu.VMEM((2, rows, lon), f32),
            pltpu.VMEM((mem * fields, rows, lon), f32),
            pltpu.VMEM(((rows + 2 * reach) * 12, SUB, 128), f32),
            pltpu.VMEM((rows + 2 * reach, SUB, 128), f32),
            pltpu.VMEM((rows * 2 * SUB, 128), f32),
            *[pltpu.VMEM(((rows + 2 * STEPS) * mem * fields * SUB, 128), f32)
              for _ in range(STEPS + 1)],
            *[pltpu.VMEM((n * 2 * (q1 - q0) * 2, SUB, 128), f32) for _, q0, q1 in plan],
            dma((2,)), dma(()), marks, marks, marks, marks, dma((len(plan),)),
            dma((2,)), dma((2,)), dma((2,)), dma((2,)),
        ],
        compiler_params=pltpu.CompilerParams(
            collective_id=0, has_side_effects=True, vmem_limit_bytes=48 * 2**20),
    )(owners, perturb.reshape(mem * fields, rows, lon), traj_store)
    return out.reshape(mem, fields, rows, lon)


def solution(mesh):
    in_specs = (
        P(("groups", "pert", "fld"), None, "lat", None),
        P(("groups", "pert"), "fld", "lat", None),
        P("groups"),
    )
    out_specs = P(("groups", "pert", "fld"), None, "lat", None)
    return jax.shard_map(
        per_device, mesh=mesh, in_specs=in_specs, out_specs=out_specs, check_vma=False
    )
```

time: 42.8 us -> 33.8 us (0.79)
  the two profiles are of different devices: /device:TPU:1 before, /device:TPU:0 now
where the time goes in v2:
time: 33.8 us; the launch traced here: 33.7 us
  Pallas kernels  29.9 us (88%)
  local copies, waits for them, and re-layouts  3.76 us (11%)
    pallas_call x1, Pallas kernels, per_device(): pl.pallas_call(functools.partial(kernel, n, nlat, mem, rows, plan), out_s...  29.9 us
    unnamed x7, local copies, waits for them, and re-layouts  3.76 us

profile of v2, /device:TPU:0, one launch (start us, length us, event | category | flops | bytes accessed | tf_op | source)
XLA Modules:
  0.0 33.7 jit_solution(11743408074682950477)
XLA Ops:
  0.0 0.0 copy-start.2
  0.0 0.7 %copy-done.2 = s32[3]{0:T(128)S(1)} copy-done((s32[3]{0:T(128)S(1)}, s32[3]{0:T(128)}, u32[]{:S(2)}) %copy-start.2) | copy-done | bytes 36
  0.7 0.0 copy-start
  0.7 1.2 %copy-done = f32[4,4,16,1024]{3,2,1,0:T(8,128)S(1)} copy-done((f32[4,4,16,1024]{3,2,1,0:T(8,128)S(1)}, f32[4,4,16,1024]{3,2,1,0:T(8,128)}, u32[]{:S(2)}) %copy-start) | copy-done | bytes 1048600
  1.9 0.0 copy-start.1
  1.9 0.9 %copy-done.1 = f32[1,2,16,1024]{3,2,1,0:T(8,128)S(1)} copy-done((f32[1,2,16,1024]{3,2,1,0:T(8,128)S(1)}, f32[1,2,16,1024]{3,2,1,0:T(8,128)}, u32[]{:S(2)}) %copy-start.1) | copy-done | bytes 131096
  2.8 29.9 %shard_map.37 = f32[16,16,1024]{2,1,0:T(8,128)S(1)} custom-call(s32[3]{0:T(128)S(1)} %copy-done.2, f32[16,16,1024]{2,1,0:T(8,128)S(1)} %bitcast.3, f32[1,2,16,1024]{3,2,1,0:T(8,128)S(1)} %copy-done.1), custom_call_target="tpu_custom_call" | custom-call | tf_op jit(solution)/shard_map/pallas_call | solution.py:379
  32.7 1.0 %copy.5 = f32[4,4,16,1024]{3,2,1,0:T(8,128)} copy(f32[4,4,16,1024]{3,2,1,0:T(8,128)S(1)} %bitcast.2) | data formatting | bytes 2097152
Async XLA Ops:
  0.0 0.7 %copy-start.2 = (s32[3]{0:T(128)S(1)}, s32[3]{0:T(128)}, u32[]{:S(2)}) copy-start(s32[3]{0:T(128)} %owners_ref.1) | copy-start | bytes 40
  0.7 1.2 %copy-start = (f32[4,4,16,1024]{3,2,1,0:T(8,128)S(1)}, f32[4,4,16,1024]{3,2,1,0:T(8,128)}, u32[]{:S(2)}) copy-start(f32[4,4,16,1024]{3,2,1,0:T(8,128)} %param.3) | copy-start | bytes 3145732
  1.9 0.9 %copy-start.1 = (f32[1,2,16,1024]{3,2,1,0:T(8,128)S(1)}, f32[1,2,16,1024]{3,2,1,0:T(8,128)}, u32[]{:S(2)}) copy-start(f32[1,2,16,1024]{3,2,1,0:T(8,128)} %traj_ref.1) | copy-start | bytes 393220

commit v3 on v2

--- a/solution.py
+++ b/solution.py
@@ -11,8 +11,8 @@
 STEPS = 6
 MESH = pl.DeviceIdType.MESH
 SUB = 8
-SPAN = 4
-PAIR = 2
+SPAN = 8
+PAIR = 4
 
 
 def chunk_plan(nlat, rows, reach):
@@ -397,7 +397,7 @@
             dma((2,)), dma((2,)), dma((2,)), dma((2,)),
         ],
         compiler_params=pltpu.CompilerParams(
-            collective_id=0, has_side_effects=True, vmem_limit_bytes=48 * 2**20),
+            collective_id=0, has_side_effects=True, vmem_limit_bytes=60 * 2**20),
     )(owners, perturb.reshape(mem * fields, rows, lon), traj_store)
     return out.reshape(mem, fields, rows, lon)
 

time: 33.8 us -> 30.3 us (0.90)
  Pallas kernels: 29.9 us -> 27.6 us
  local copies, waits for them, and re-layouts: 3.76 us -> 2.31 us
    pallas_call x1, Pallas kernels: 29.9 us -> 27.6 us  [per_device(): pl.pallas_call(functools.partial(kernel, n, nlat, mem, rows, plan), out_s...]
    unnamed x7 -> x1, local copies, waits for them, and re-layouts: 3.76 us -> 2.31 us
where the time goes in v3:
time: 30.3 us; the launch traced here: 29.9 us
  Pallas kernels  27.6 us (91%)
  local copies, waits for them, and re-layouts  2.31 us (8%)
    pallas_call x1, Pallas kernels, per_device(): pl.pallas_call(functools.partial(kernel, n, nlat, mem, rows, plan), out_s...  27.6 us
    unnamed x1, local copies, waits for them, and re-layouts  2.31 us

profile of v3, /device:TPU:0, one launch (start us, length us, event | category | flops | bytes accessed | tf_op | source)
XLA Modules:
  0.0 29.9 jit_solution(10161873136104740274)
XLA Ops:
  0.0 27.6 %shard_map.37 = f32[16,16,1024]{2,1,0:T(8,128)} custom-call(s32[3]{0:T(128)} %owners_ref.1, f32[16,16,1024]{2,1,0:T(8,128)} %bitcast.3, f32[1,2,16,1024]{3,2,1,0:T(8,128)} %traj_ref.1), custom_call_target="tpu_custom_call" | custom-call | tf_op jit(solution)/shard_map/pallas_call | solution.py:379
  27.6 2.3 %copy.5 = f32[4,4,16,1024]{3,2,1,0:T(8,128)} copy(f32[4,4,16,1024]{3,2,1,0:T(8,128)} %bitcast.2) | data formatting | bytes 2097152
